TPU v7x, 32 devices: a whole 2x2x4 slice. The times are simulated.
32 devices in a mesh: gx: 8 (over z, core), gy: 4 (over y, x).
Axes of the slice: x: 2, y: 2, z: 4, core: 2. Of those that a mesh axis runs over, the one named last changes fastest.
Arguments:
- source: float32 [64, 512, 256], P('gx', 'gy'), may hold values from -8 to 8
- density: float32 [64, 512, 256], P('gx', 'gy'), may hold values from 0.08 to 1.7
Outputs:
- pressure: float32 [64, 512, 256], P('gx', 'gy')
- residual: float32 [64, 512, 256], P('gx', 'gy')
All inputs are finite; a program needn't handle non-finite values.
Results may differ from a plain program's by a relative error of at most 0.00021.
Values sent between devices are 32-bit elements; how exact they have to be, the bound alone decides.
No kernel may reach another device: no remote copies, remote signals or barrier semaphores. Data moves between devices by JAX's collectives and lax.ppermute only.
A program may use at most 64 MiB of HBM per device.

v0:
```python
import functools

import jax
import jax.numpy as jnp
from jax import lax
from jax.experimental import pallas as pl
from jax.experimental.pallas import tpu as pltpu
from jax.sharding import PartitionSpec as P


TILE = 8
LANES = 128
OFF = 16
DEEP = 3
ROWS = 5
STEP = 2
HALF = TILE // 2
PART = 16
SUMS = 5
MIB = 1 << 20
VMEM = pltpu.VMEM


def swaps(nx, ny):
    at = lambda x, y: x * ny + y
    near, far, ynear, yfar = [], [], [], []
    for x in range(nx):
        for y in range(ny):
            near.append((at(x, y), at(x ^ 1, y)))
            other = x - 1 if x % 2 == 0 else x + 1
            inside = 0 <= other < nx
            far.append((at(x, y), at(other, y) if inside else at(x, (y + ny // 2) % ny)))
            ynear.append((at(x, y), at(x, y ^ 1)))
            beside = y - 1 if y % 2 == 0 else y + 1
            within = 0 <= beside < ny
            yfar.append((at(x, y), at(x, beside) if within else at(x ^ 1, y)))
    return near, far, ynear, yfar


def position(sizes):
    ix, iy = lax.axis_index("gx"), lax.axis_index("gy")
    flags = (ix % 2 == 1, iy % 2 == 1, ix > 0, ix < sizes[0] - 1, iy > 0, iy < sizes[1] - 1)
    return [jnp.where(f, 1, 0) for f in flags]


def load_far_kernel(sizes, dens_hbm, src_hbm, far, dens, src, tall, sems):
    par = position(sizes)
    nx, ny, nz = dens_hbm.shape
    xodd = par[0] == 1
    copies = []
    for k in range(3):
        at = jnp.where(xodd, nx - 1 - k, k)
        for i, (a, b) in enumerate(((dens_hbm, dens), (src_hbm, src))):
            if k < 2 or a is dens_hbm:
                copies.append(pltpu.make_async_copy(a.at[pl.ds(at, 1)], b.at[pl.ds(k, 1)], sems.at[2 * k + i]))
    for copy in copies:
        copy.start()
    for copy in copies:
        copy.wait()
    far[0] = dens[0]
    far[1] = dens[1]
    far[2] = src[0]
    second = dens[1]
    put_plane(tall, 0, slice(TILE, TILE + ny), 0.5 * second)
    lane = lax.broadcasted_iota(jnp.int32, (TILE, LANES), 1)
    inner, first = lane < LANES - 1, lane == 0
    for r in range(0, ny, TILE):
        here = pl.ds(r + TILE, TILE)
        c = [tall[0, h, here] for h, _ in halves(nz)]
        z_up, z_down, _ = depth_weights(c, inner, first)
        for h, lanes in halves(nz):
            beside = [0.5 * dens[k, pl.ds(r, TILE), lanes] for k in (0, 2)]
            beside += [tall[0, h, pl.ds(r + TILE + 1, TILE)], tall[0, h, pl.ds(r + TILE - 1, TILE)]]
            w = [1.0 / (c[h] + v) for v in beside]
            s = lax.rsqrt((w[0] + w[1]) + (w[2] + w[3]) + (z_up[h] + z_down[h]))
            far[3, pl.ds(r, TILE), lanes] = s * (s * src[1, pl.ds(r, TILE), lanes])


def pack_kernel(sizes, dens, src, near, xs, dg):
    par = position(sizes)
    nx, ny, _ = dens.shape
    xodd, yodd = par[0] == 1, par[1] == 1
    d, s = jnp.where(xodd, 0, nx - 3), jnp.where(xodd, 0, nx - 2)
    for k in range(3):
        near[k] = dens[d + k]
    for k in range(2):
        near[3 + k] = src[s + k]
    for j in range(ROWS):
        ref, at = (dens, j) if j < DEEP else (src, j - DEEP)
        down, up = ref[:, at, :], ref[:, ny - 1 - at, :]
        xs[j] = jnp.where(yodd, down, up)
        dg[j] = jnp.where(yodd, up, down)


def corner_kernel(sizes, rxs, rdg, dens, src, far, near):
    par = position(sizes)
    xodd, yodd = par[0] == 1, par[1] == 1
    nx, ny, _ = dens.shape
    for out, backward in ((far, xodd), (near, jnp.logical_not(xodd))):
        at = [jnp.where(backward, nx - 1 - k, k) for k in range(3)]
        for k in range(2):
            for j in range(ROWS):
                a, b = rxs[j, pl.ds(at[k], 1), :], rdg[j, pl.ds(at[k], 1), :]
                out[k, j:j + 1] = jnp.where(yodd, a, b)
                out[2 + k, j:j + 1] = jnp.where(yodd, b, a)
        for side, row in ((0, 0), (1, ny - 1)):
            out[2 * side + 1, ROWS:ROWS + 1] = dens[at[2], row:row + 1]
            out[2 * side + 1, ROWS + 1:ROWS + 2] = src[at[1], row:row + 1]


class Stores:
    def __init__(self, depth):
        self.depth, self.held = depth, []

    def put(self, items):
        self.held.append(items)
        if len(self.held) > self.depth:
            self.flush(1)

    def flush(self, count=None):
        for items in self.held[:count]:
            for ref, at, value in items:
                ref[at] = value
        self.held = [] if count is None else self.held[count:]


def halves(nz):
    return [(h, slice(h * LANES, (h + 1) * LANES)) for h in range(nz // LANES)]


def loop(count, step):
    def body(k, carry):
        step(k)
        return carry

    lax.fori_loop(0, count, body, 0)


def put_plane(ref, e, rows, value):
    for h, lanes in halves(value.shape[-1]):
        ref[e, h, rows] = value[:, lanes]


def put_row(dx, sx, planes, ny, j, low, high):
    ref, depth = (dx, j) if j < DEEP else (sx, j - DEEP)
    if j < DEEP:
        low, high = 0.5 * low, 0.5 * high
    for value, at in ((low, OFF - 1 - depth), (high, OFF + ny + depth)):
        for h, lanes in halves(value.shape[-1]):
            ref[planes, h, at, :] = value[:, lanes]


def depth_weights(c, inner, first):
    nh = len(c)
    turned = [pltpu.roll(v, LANES - 1, 1) for v in c]
    z_up, z_in = [], []
    for h in range(nh):
        w = 1.0 / (c[h] + jnp.where(inner, turned[h], turned[h + 1] if h + 1 < nh else 0.0))
        z_up.append(w)
        z_in.append(w if h + 1 < nh else jnp.where(inner, w, 0.0))
    back = [pltpu.roll(v, 1, 1) for v in z_in]
    z_down = [jnp.where(first, back[h - 1] if h else 1.0 / c[0], back[h]) for h in range(nh)]
    return z_up, z_down, z_in


def weigh(dx, sx, wx, wy, wz, sc, g0, lo, count, tiles, unroll=1):
    nh = dx.shape[1]
    lane = lax.broadcasted_iota(jnp.int32, (TILE, LANES), 1)
    inner, first = lane < LANES - 1, lane == 0
    for r in tiles:
        for h in range(nh):
            wx[lo - 1, h, pl.ds(r, TILE)] = 1.0 / (dx[lo - 1, h, pl.ds(r, TILE)] + dx[lo, h, pl.ds(r, TILE)])

    def plane(k, carry):
        e = lo + k
        stores = Stores(1)
        for r in tiles:
            here = pl.ds(r, TILE)
            c = [dx[e, h, here] for h in range(nh)]
            beside = [(dx[e + 1, h, here], wx[e - 1, h, here], dx[e, h, pl.ds(r + 1, TILE)], dx[e, h, pl.ds(r - 1, TILE)], sx[e, h, here])
                      for h in range(nh)]
            z_up, z_down, z_in = depth_weights(c, inner, first)
            items = [(wz, (e, h, here), z_in[h]) for h in range(nh)]
            for h in range(nh):
                above, x_down, after, before, source = beside[h]
                x_up = 1.0 / (c[h] + above)
                y_up = 1.0 / (c[h] + after)
                y_down = 1.0 / (c[h] + before)
                diag = (x_up + x_down) + (y_up + y_down) + (z_up[h] + z_down[h])
                s = lax.rsqrt(diag)
                items += [(wx, (e, h, here), x_up), (wy, (e, h, here), y_up), (sc, (e, h, here), s), (g0, (e, h, here), s * (s * source))]
            stores.put(items)
        stores.flush()
        return carry

    lax.fori_loop(0, count, plane, 0, unroll=unroll)


def couple(g, wx, wy, wz, e, r, nh, inner, first):
    here = pl.ds(r, TILE)
    c = [g[e, h, here] for h in range(nh)]
    w = [wz[e, h, here] for h in range(nh)]
    ahead = [pltpu.roll(v, LANES - 1, 1) for v in c]
    behind = [pltpu.roll(a * b, 1, 1) for a, b in zip(w, c)]
    out = []
    for h in range(nh):
        t = wx[e, h, here] * g[e + 1, h, here] + wx[e - 1, h, here] * g[e - 1, h, here]
        t = t + (wy[e, h, here] * g[e, h, pl.ds(r + 1, TILE)] + wy[e, h, pl.ds(r - 1, TILE)] * g[e, h, pl.ds(r - 1, TILE)])
        after = jnp.where(inner, ahead[h], ahead[h + 1]) if h + 1 < nh else ahead[h]
        before = jnp.where(first, behind[h - 1], behind[h])
        out.append(t + (w[h] * after + before))
    return out


def apply_first(sx, wx, wy, wz, sc, g0, g1, w0, lo, count, tiles, unroll=1):
    nh = sx.shape[1]
    lane = lax.broadcasted_iota(jnp.int32, (TILE, LANES), 1)
    inner, first = lane < LANES - 1, lane == 0

    def plane(k, carry):
        e = lo + k
        stores = Stores(1)
        for r in tiles:
            here = pl.ds(r, TILE)
            t = couple(g0, wx, wy, wz, e, r, nh, inner, first)
            items = []
            for h in range(nh):
                s = sc[e, h, here]
                v = s * sx[e, h, here] - s * t[h]
                items += [(w0, (e, h, here), v), (g1, (e, h, here), s * v)]
            stores.put(items)
        stores.flush()
        return carry

    lax.fori_loop(0, count, plane, 0, unroll=unroll)


def clear_rows(par, g1):
    _, nh, rows, _ = g1.shape
    zero = jnp.zeros((TILE, LANES), jnp.float32)
    for flag, at in ((par[4], OFF - TILE), (par[5], rows - OFF)):

        @pl.when(flag == 0)
        def _():
            for k in range(g1.shape[0]):
                for h in range(nh):
                    g1[k, h, pl.ds(at, TILE)] = zero


def clear_plane(g1, e, has, tiles):
    zero = jnp.zeros((TILE, LANES), jnp.float32)

    @pl.when(has == 0)
    def _():
        for r in tiles:
            for h in range(g1.shape[1]):
                g1[e, h, pl.ds(r, TILE)] = zero


def apply_second(sx, wx, wy, wz, sc, g1, w0, n0, lo, count, tiles, sums, unroll=1, edges=False):
    row = lax.broadcasted_iota(jnp.int32, (TILE, LANES), 0)
    nh = sx.shape[1]
    lane = lax.broadcasted_iota(jnp.int32, (TILE, LANES), 1)
    inner, first = lane < LANES - 1, lane == 0

    def plane(k, sums):
        e = lo + k
        sums = list(sums)
        stores = Stores(2)
        for r in tiles:
            t = couple(g1, wx, wy, wz, e, r, nh, inner, first)
            for h in range(nh):
                s = sc[e, h, pl.ds(r, TILE)]
                a = s * sx[e, h, pl.ds(r, TILE)]
                b = w0[e, h, pl.ds(r, TILE)]
                c = b - s * t[h]
                stores.put([(n0, (e, h, pl.ds(r, TILE)), c)])
                if edges:
                    own = row >= HALF if r < OFF else row < HALF
                    a, b, c = (jnp.where(own, v, 0.0) for v in (a, b, c))
                for i, term in enumerate((a * a, b * a, b * b, c * b, c * a)):
                    sums[i] = sums[i] + term
        stores.flush()
        return tuple(sums)

    return lax.fori_loop(0, count, plane, tuple(sums), unroll=unroll)


def beyond(nx, upper, depth):
    return jnp.where(upper, nx + DEEP - 1 + depth, DEEP - depth)


def put_corners(dx, sx, corners, upper, has_down, has_up):
    nx, ny = dx.shape[0] - 2 * DEEP, dx.shape[2] - 2 * OFF
    for k in range(2):
        e = beyond(nx, upper, k + 1)
        for j in range(ROWS):
            low, high = corners[k, j:j + 1], corners[2 + k, j:j + 1]
            put_row(dx, sx, pl.ds(e, 1), ny, j, jnp.where(has_down, low, 0.0), jnp.where(has_up, high, 0.0))


def row_tiles(first, last):
    tiles = list(range(first, last - TILE + 1, TILE))
    if tiles[-1] + TILE < last:
        tiles.append(last - TILE)
    return [OFF + r for r in tiles]


def edge_tiles(ny):
    return [OFF - HALF, OFF + ny - HALF]


def near_side(par):
    xodd = par[0] == 1
    return jnp.where(xodd, 1, 4), jnp.where(xodd, 2, 5), jnp.where(xodd, 3, 6), jnp.where(xodd, par[2], par[3])


def inner_kernel(sizes, dens, src, dx, sx, wx, wy, wz, sc, g0, g1, w0, n0, mom):
    nx, ny, _ = dens.shape
    own = slice(OFF, OFF + ny)

    def fill(k):
        put_plane(dx, k + DEEP, own, 0.5 * dens[k])
        put_plane(sx, k + DEEP, own, src[k])

    loop(nx, fill)
    weigh(dx, sx, wx, wy, wz, sc, g0, DEEP + 1, nx - 2, row_tiles(1, ny - 1), unroll=2)
    apply_first(sx, wx, wy, wz, sc, g0, g1, w0, DEEP + 2, nx - 4, row_tiles(2, ny - 2), unroll=4)
    zero = jnp.zeros((TILE, LANES), jnp.float32)
    sums = apply_second(sx, wx, wy, wz, sc, g1, w0, n0, DEEP + 3, nx - 6, row_tiles(HALF, ny - HALF), (zero,) * SUMS)
    for i in range(SUMS):
        mom[i] = sums[i]


def beside_kernel(sizes, near, *refs):
    dx, sx, wx, wy, wz, sc, g0, g1, w0 = refs[9:]
    par = position(sizes)
    ny = near.shape[1]
    nx = dx.shape[0] - 2 * DEEP
    xodd = par[0] == 1
    has = near_side(par)[3]
    has_near = has == 1
    own = slice(OFF, OFF + ny)
    near_third, near_beyond = jnp.where(xodd, 0, nx + 3), jnp.where(xodd, 1, nx + 3)
    loop(3, lambda k: put_plane(dx, near_third + k, own, jnp.where(has_near, 0.5 * near[k], 0.0)))
    loop(2, lambda k: put_plane(sx, near_beyond + k, own, jnp.where(has_near, near[3 + k], 0.0)))
    weigh(dx, sx, wx, wy, wz, sc, g0, jnp.where(xodd, 1, nx + 2), 3, row_tiles(1, ny - 1), unroll=1)
    apply_first(sx, wx, wy, wz, sc, g0, g1, w0, jnp.where(xodd, 2, nx + 1), 3, row_tiles(2, ny - 2), unroll=3)
    clear_plane(g1, jnp.where(xodd, 2, nx + 3), has, row_tiles(2, ny - 2))


def inner_second_kernel(sizes, sx, wx, wy, wz, sc, g1, w0, part, n0_in, n0, mom):
    par = position(sizes)
    nx, ny = sx.shape[0] - 2 * DEEP, sx.shape[2] - 2 * OFF
    third = jnp.where(par[0] == 1, DEEP, nx)
    sums = apply_second(sx, wx, wy, wz, sc, g1, w0, n0, third, 3, row_tiles(HALF, ny - HALF), [part[i] for i in range(SUMS)], unroll=3)
    for i in range(SUMS):
        mom[i] = sums[i]


def edge_kernel(sizes, rxs, rdg, rnc, part, *refs):
    par = position(sizes)
    mom, dx, sx, wx, wy, wz, sc, g0, g1, w0, n0 = refs[10:]
    nx = dx.shape[0] - 2 * DEEP
    ny = dx.shape[2] - 2 * OFF
    xodd, yodd = par[0] == 1, par[1] == 1
    first, second, third, has = near_side(par)
    has_near, has_down, has_up = has == 1, par[4] == 1, par[5] == 1
    for j in range(ROWS):
        a, b = rxs[j], rdg[j]
        low, high = jnp.where(yodd, a, b), jnp.where(yodd, b, a)
        put_row(dx, sx, pl.ds(DEEP, nx), ny, j, jnp.where(has_down, low, 0.0), jnp.where(has_up, high, 0.0))
    put_corners(dx, sx, rnc, jnp.logical_not(xodd), jnp.logical_and(has_near, has_down), jnp.logical_and(has_near, has_up))
    weigh(dx, sx, wx, wy, wz, sc, g0, first, nx + 1, edge_tiles(ny), unroll=9)
    apply_first(sx, wx, wy, wz, sc, g0, g1, w0, second, nx - 1, edge_tiles(ny), unroll=7)
    clear_plane(g1, jnp.where(xodd, 2, nx + 3), has, edge_tiles(ny))
    clear_rows(par, g1)
    sums = apply_second(sx, wx, wy, wz, sc, g1, w0, n0, third, nx - 3, edge_tiles(ny), [part[i] for i in range(SUMS)], unroll=5, edges=True)
    for i in range(SUMS):
        mom[i] = sums[i]


def far_side(par, nx):
    xodd = par[0] == 1
    return jnp.where(xodd, nx + 2, 2), jnp.where(xodd, nx + 1, 2), jnp.where(xodd, nx, 3), jnp.where(xodd, par[3], par[2])


def far_kernel(sizes, far, part, *refs):
    mom, dx, sx, wx, wy, wz, sc, g0, g1, w0, n0 = refs[10:]
    par = position(sizes)
    ny = far.shape[1]
    nx = dx.shape[0] - 2 * DEEP
    first, second, third, has = far_side(par, nx)
    has_far = has == 1
    own = slice(OFF, OFF + ny)
    e1, e2 = (beyond(nx, par[0] == 1, d) for d in (1, 2))
    put_plane(dx, e1, own, jnp.where(has_far, 0.5 * far[0], 0.0))
    put_plane(dx, e2, own, jnp.where(has_far, 0.5 * far[1], 0.0))
    put_plane(sx, e1, own, jnp.where(has_far, far[2], 0.0))
    put_plane(g0, e2, own, jnp.where(has_far, far[3], 0.0))
    weigh(dx, sx, wx, wy, wz, sc, g0, first, 2, row_tiles(1, ny - 1))
    apply_first(sx, wx, wy, wz, sc, g0, g1, w0, second, 3, row_tiles(2, ny - 2), unroll=3)
    clear_plane(g1, e1, has, row_tiles(2, ny - 2))
    sums = apply_second(sx, wx, wy, wz, sc, g1, w0, n0, third, 3, row_tiles(HALF, ny - HALF), [part[i] for i in range(SUMS)], unroll=3)
    for i in range(SUMS):
        mom[i] = sums[i]


def far_edge_kernel(sizes, rfc, part, *refs):
    mom, dx, sx, wx, wy, wz, sc, g0, g1, w0, n0 = refs[10:]
    par = position(sizes)
    nx, ny = dx.shape[0] - 2 * DEEP, dx.shape[2] - 2 * OFF
    nz = rfc.shape[-1]
    xodd = par[0] == 1
    first_plane, second, third, has = far_side(par, nx)
    has_far = has == 1
    has_down, has_up = jnp.logical_and(has_far, par[4] == 1), jnp.logical_and(has_far, par[5] == 1)
    e1, e2 = (beyond(nx, xodd, d) for d in (1, 2))
    put_corners(dx, sx, rfc, xodd, has_down, has_up)
    lane = lax.broadcasted_iota(jnp.int32, (TILE, LANES), 1)
    row = lax.broadcasted_iota(jnp.int32, (TILE, LANES), 0)
    inner, first = lane < LANES - 1, lane == 0
    for side, r in ((0, OFF), (1, OFF + ny - TILE)):
        here = pl.ds(r, TILE)
        c = [dx[e2, h, here] for h, _ in halves(nz)]
        z_up, z_down, _ = depth_weights(c, inner, first)
        for h, lanes in halves(nz):
            density = jnp.where(has_far, 0.5 * rfc[2 * side + 1, ROWS:ROWS + 1, lanes], 0.0)
            source = jnp.where(has_far, rfc[2 * side + 1, ROWS + 1:ROWS + 2, lanes], 0.0)
            w = [1.0 / (c[h] + v) for v in (density, dx[e1, h, here], dx[e2, h, pl.ds(r + 1, TILE)], dx[e2, h, pl.ds(r - 1, TILE)])]
            s = lax.rsqrt((w[0] + w[1]) + (w[2] + w[3]) + (z_up[h] + z_down[h]))
            g0[e2, h, here] = jnp.where(row == side * (TILE - 1), s * (s * source), g0[e2, h, here])
    weigh(dx, sx, wx, wy, wz, sc, g0, first_plane, 2, edge_tiles(ny), unroll=2)
    apply_first(sx, wx, wy, wz, sc, g0, g1, w0, second, 3, edge_tiles(ny), unroll=3)
    clear_plane(g1, e1, has, edge_tiles(ny))
    clear_rows(par, g1)
    sums = apply_second(sx, wx, wy, wz, sc, g1, w0, n0, third, 3, edge_tiles(ny), [part[i] for i in range(SUMS)], unroll=3, edges=True)
    place = lax.broadcasted_iota(jnp.int32, (1, LANES), 1) // PART
    out = jnp.zeros((1, LANES), jnp.float32)
    for k, v in enumerate(sums):
        p = jnp.sum(v, axis=0, keepdims=True)
        width = LANES // 2
        while width >= PART:
            p = p + pltpu.roll(p, width, 1)
            width //= 2
        out = jnp.where(place == k, p, out)
    mom[...] = out


def last_kernel(mom, sx, sc, w0, n0, p_out, r_out, p_buf, r_buf, sems):
    place = lax.broadcasted_iota(jnp.int32, mom.shape, 1) // PART
    m = mom[...]

    def whole(v):
        return jnp.sum(jnp.sum(v, axis=0, keepdims=True), axis=1, keepdims=True)

    def lanes(k):
        return pltpu.roll(m, (LANES - k * PART) % LANES, 1) if k else m

    head = place == 0
    m0, m1, m2, m3, m4 = (jnp.where(head, lanes(k), 0.0) for k in range(SUMS))
    gamma0 = whole(m0)
    delta0 = whole(m1)
    a0 = gamma0 / delta0
    gamma1 = whole(m0 - a0 * (m1 + m1 - a0 * m2))
    delta1 = whole(m1 - a0 * (m4 + m2 - a0 * m3))
    b1 = gamma1 / gamma0
    a1 = gamma1 / (delta1 - b1 * gamma1 / a0)
    nx, ny, nz = p_out.shape
    c = jnp.broadcast_to(a0 + (a1 + a1 * b1), (TILE, LANES))
    d = jnp.broadcast_to(a0 * a1, (TILE, LANES))

    def out(i):
        here = pl.ds(i * STEP, STEP)
        return (pltpu.make_async_copy(p_buf.at[here], p_out.at[here], sems.at[0, i]),
                pltpu.make_async_copy(r_buf.at[here], r_out.at[here], sems.at[1, i]))

    def group(i, carry):
        for k in range(STEP):
            plane = i * STEP + k
            e = plane + DEEP
            stores = Stores(2)
            for r in range(0, ny, TILE):
                here, there = pl.ds(OFF + r, TILE), pl.ds(r, TILE)
                items = []
                for h, at in halves(nz):
                    s, q, v0, v1 = sc[e, h, here], sx[e, h, here], w0[e, h, here], n0[e, h, here]
                    r0 = s * q
                    items.append((p_buf, (plane, there, at), s * (c * r0 - d * v0)))
                    items.append((r_buf, (plane, there, at), r0 - c * v0 + d * v1))
                stores.put(items)
            stores.flush()
        for copy in out(i):
            copy.start()
        return carry

    lax.fori_loop(0, nx // STEP, group, 0)
    for i in range(nx // STEP):
        for copy in out(i):
            copy.wait()


def shards(nx_dev, ny_dev, source, density):
    both = ("gx", "gy")
    near_pairs, far_pairs, ynear_pairs, yfar_pairs = swaps(nx_dev, ny_dev)
    nx, ny, nz = density.shape
    sizes = (nx_dev, ny_dev)
    vmem = pl.BlockSpec(memory_space=VMEM)
    hbm = pl.BlockSpec(memory_space=pltpu.HBM)

    def call(body, n_in, outs, limit, **more):
        return pl.pallas_call(
            functools.partial(body, sizes), out_shape=outs, in_specs=[vmem] * n_in, out_specs=jax.tree.map(lambda _: vmem, outs),
            compiler_params=pltpu.CompilerParams(vmem_limit_bytes=limit * MIB), **more,
        )

    def send(value, pairs):
        return lax.ppermute(value, both, pairs)

    few, planes, rows = (VMEM(v, jnp.float32) for v in ((4, ny, nz), (5, ny, nz), (ROWS, nx, nz)))
    far = pl.pallas_call(
        functools.partial(load_far_kernel, sizes), out_shape=few, in_specs=[hbm] * 2, out_specs=vmem, name="load_far_kernel",
        scratch_shapes=[VMEM((3, ny, nz), jnp.float32), VMEM((2, ny, nz), jnp.float32),
                        VMEM((1, nz // LANES, ny + 2 * TILE, LANES), jnp.float32), pltpu.SemaphoreType.DMA((5,))],
        compiler_params=pltpu.CompilerParams(vmem_limit_bytes=8 * MIB),
    )(*(pltpu.with_memory_space_constraint(v, pltpu.HBM) for v in (density, source)))
    dens, src = density, source
    near, xs, dg = call(pack_kernel, 2, (planes, rows, rows), 4)(dens, src)
    far = send(far, far_pairs)
    near = send(near, near_pairs)
    rxs = send(xs, ynear_pairs)
    rdg = send(dg, yfar_pairs)
    corner = VMEM((4, TILE, nz), jnp.float32)
    rfc, rnc = call(corner_kernel, 4, (corner, corner), 4)(rxs, rdg, dens, src)
    rfc = send(rfc, far_pairs)
    rnc = send(rnc, near_pairs)

    ext = VMEM((nx + 2 * DEEP, nz // LANES, ny + 2 * OFF, LANES), jnp.float32)
    sums = VMEM((SUMS, TILE, LANES), jnp.float32)
    *held, n0, part = call(inner_kernel, 2, (ext,) * 10 + (sums,), 8)(dens, src)
    held = call(beside_kernel, 10, (ext,) * 9, 8, input_output_aliases={1 + k: k for k in range(9)})(near, *held)
    dx, sx, wx, wy, wz, sc, g0, g1, w0 = held
    n0, part = call(inner_second_kernel, 9, (ext, sums), 8, input_output_aliases={8: 0})(sx, wx, wy, wz, sc, g1, w0, part, n0)
    held = (*held, n0)
    part, *held = call(edge_kernel, 14, (sums,) + (ext,) * 10, 8, input_output_aliases={4 + k: 1 + k for k in range(10)})(
        rxs, rdg, rnc, part, *held)
    part, *held = call(far_kernel, 12, (sums,) + (ext,) * 10, 8, input_output_aliases={2 + k: 1 + k for k in range(10)})(
        far, part, *held)
    mom, *held = call(far_edge_kernel, 12, (VMEM((1, LANES), jnp.float32),) + (ext,) * 10, 8, input_output_aliases={2 + k: 1 + k for k in range(10)})(
        rfc, part, *held)
    dx, sx, wx, wy, wz, sc, g0, g1, w0, n0 = held

    n = nx_dev * ny_dev
    sent = jnp.broadcast_to(mom[None], (n, 1, LANES))
    got = lax.all_to_all(sent, both, 0, 0, tiled=True).reshape(n, LANES)
    whole = jax.ShapeDtypeStruct(density.shape, jnp.float32)
    plane = VMEM(density.shape, jnp.float32)
    return pl.pallas_call(
        last_kernel, out_shape=(whole, whole), in_specs=[vmem] * 5, out_specs=(hbm, hbm), name="last_kernel",
        scratch_shapes=[plane, plane, pltpu.SemaphoreType.DMA((2, nx))],
        compiler_params=pltpu.CompilerParams(vmem_limit_bytes=8 * MIB),
    )(got, sx, sc, w0, n0)


def solution(mesh):
    spec = P("gx", "gy", None)
    body = functools.partial(shards, mesh.shape["gx"], mesh.shape["gy"])
    return jax.shard_map(body, mesh=mesh, in_specs=(spec, spec), out_specs=(spec, spec), check_vma=False)
```

profile of v0, /device:TPU:0, one launch (start us, length us, event | category | flops | bytes accessed | tf_op | source)
XLA Modules:
  0.0 34.5 jit_solution(11141573267919175263)
XLA Ops:
  0.6 0.0 copy-start
  0.6 1.2 %copy-done = f32[8,128,256]{2,1,0:T(8,128)S(1)} copy-done((f32[8,128,256]{2,1,0:T(8,128)S(1)}, f32[8,128,256]{2,1,0:T(8,128)}, u32[]{:S(2)}) %copy-start) | copy-done | bytes 1048600
  1.9 0.0 copy-start.2
  1.9 1.2 %copy-done.2 = f32[8,128,256]{2,1,0:T(8,128)S(1)} copy-done((f32[8,128,256]{2,1,0:T(8,128)S(1)}, f32[8,128,256]{2,1,0:T(8,128)}, u32[]{:S(2)}) %copy-start.2) | copy-done | bytes 1048600
  3.1 0.0 copy-start.1
  3.1 0.0 copy-start.3
  3.1 0.1 shard_map.41
  3.2 0.6 %collective-permute-start.5 = (f32[5,128,256]{2,1,0:T(8,128)S(1)}, f32[5,128,256]{2,1,0:T(8,128)S(1)}, u32[]{:S(2)}, u32[]{:S(2)}) collective-permute-start(f32[5,128,256]{2,1,0:T(8,128)S(1)} %get-tuple-element.60), channel_id=1, source_target_pairs={{0,4},{1,5},{2,6},{3,7},{4,0},{5,1},{6,2},{7,3},{8,12},{9,13},{10,... | collective-permute-start | bytes 1966088 | tf_op jit(solution)/shard_map/ppermute | solution.py:518
  3.7 1.4 %load_far_kernel.1 = f32[4,128,256]{2,1,0:T(8,128)S(1)} custom-call(f32[8,128,256]{2,1,0:T(8,128)} %dens.5, f32[8,128,256]{2,1,0:T(8,128)} %src.5), custom_call_target="tpu_custom_call" | custom-call | tf_op jit(solution)/shard_map/load_far_kernel/pallas_call | solution.py:521
  5.2 2.7 %collective-permute-start.3 = (f32[4,128,256]{2,1,0:T(8,128)S(1)}, f32[4,128,256]{2,1,0:T(8,128)S(1)}, u32[]{:S(2)}, u32[]{:S(2)}) collective-permute-start(f32[4,128,256]{2,1,0:T(8,128)S(1)} %load_far_kernel.1), channel_id=1, source_target_pairs={{0,2},{1,3},{2,0},{3,1},{4,8},{5,9},{6,10},{7,11},{8,4},{9,5},{10,... | collective-permute-start | bytes 1572872 | tf_op jit(solution)/shard_map/ppermute | solution.py:518
  7.9 1.5 %collective-permute-start = (f32[5,8,256]{2,1,0:T(8,128)S(1)}, f32[5,8,256]{2,1,0:T(8,128)S(1)}, u32[]{:S(2)}, u32[]{:S(2)}) collective-permute-start(f32[5,8,256]{2,1,0:T(8,128)S(1)} %get-tuple-element.56), channel_id=1, source_target_pairs={{0,1},{1,0},{2,3},{3,2},{4,5},{5,4},{6,7},{7,6},{8,9},{9,8},{10,11... | collective-permute-start | bytes 122888 | tf_op jit(solution)/shard_map/ppermute | solution.py:518
  9.4 0.0 collective-permute-start.1
  9.4 2.5 %collective-permute-done.rxs = f32[5,8,256]{2,1,0:T(8,128)S(1)} collective-permute-done((f32[5,8,256]{2,1,0:T(8,128)S(1)}, f32[5,8,256]{2,1,0:T(8,128)S(1)}, u32[]{:S(2)}, u32[]{:S(2)}) %collective-permute-start) | collective-permute-done | bytes 40992 | tf_op jit(solution)/shard_map/ppermute | solution.py:518
  11.9 0.0 collective-permute-done.1.rdg
  11.9 0.0 copy-done.1
  11.9 0.0 copy-done.3
  11.9 0.1 shard_map.42
  12.0 0.1 collective-permute-start.4
  12.0 3.4 %collective-permute-start.2 = (f32[4,8,256]{2,1,0:T(8,128)S(1)}, f32[4,8,256]{2,1,0:T(8,128)S(1)}, u32[]{:S(2)}, u32[]{:S(2)}) collective-permute-start(f32[4,8,256]{2,1,0:T(8,128)S(1)} %get-tuple-element.58), channel_id=1, source_target_pairs={{0,2},{1,3},{2,0},{3,1},{4,8},{5,9},{6,10},{7,11},{8,4},{9,5},{10,... | collective-permute-start | bytes 98312 | tf_op jit(solution)/shard_map/ppermute | solution.py:518
  15.4 2.0 %shard_map.43 = (f32[14,2,160,128]{3,2,1,0:T(8,128)S(1)}, f32[14,2,160,128]{3,2,1,0:T(8,128)S(1)}, f32[14,2,160,128]{3,2,1,0:T(8,128)S(1)}, f32[14,2,160,128]{3,...) custom-call(f32[8,128,256]{2,1,0:T(8,128)S(1)} %copy-done.1, ...), custom_call_target="tpu_custom_call" | custom-call | tf_op jit(solution)/shard_map/pallas_call | solution.py:540
  17.4 0.0 collective-permute-done.5.near
  17.4 1.2 %shard_map.44 = (f32[14,2,160,128]{3,2,1,0:T(8,128)S(1)}, f32[14,2,160,128]{3,2,1,0:T(8,128)S(1)}, f32[14,2,160,128]{3,2,1,0:T(8,128)S(1)}, f32[14,2,160,128]{3,...) custom-call(f32[5,128,256]{2,1,0:T(8,128)S(1)} %collective-permute-d, ...), custom_call_target="tpu_custom_call", output_to_operand_aliasing={{0}: (1, {}), {1}: (2, {}), {2}: (3, {}), {3}: (4, {}), {4}... | custom-call | tf_op jit(solution)/shard_map/pallas_call | solution.py:541
  18.6 0.5 %shard_map.45 = (f32[14,2,160,128]{3,2,1,0:T(8,128)S(1)}, f32[5,8,128]{2,1,0:T(8,128)S(1)}) custom-call(f32[14,2,160,128]{3,2,1,0:T(8,128)S(1)} %get-tuple-element.70.sx.refs_1_, f32[14,2,160,128]{3,2,1,0:T(8,128)S(1)} %get-tuple-element.71.wx.refs_2_, f32[14,2,160,128]{3,2,1,0:T(8,128)S(1)} %get-tuple-element.72.wy.refs_3_, ...), custom_call_target="tpu_custom_call", output_to_operand_aliasing={{0}: (8, {})} | custom-call | tf_op jit(solution)/shard_map/pallas_call | solution.py:543
  19.2 0.0 collective-permute-done.4.rnc
  19.2 0.7 %shard_map.46 = (f32[5,8,128]{2,1,0:T(8,128)S(1)}, f32[14,2,160,128]{3,2,1,0:T(8,128)S(1)}, f32[14,2,160,128]{3,2,1,0:T(8,128)S(1)}, f32[14,2,160,128]{3,2,1,0:T...) custom-call(f32[5,8,256]{2,1,0:T(8,128)S(1)} %collective-permute-don, ...), custom_call_target="tpu_custom_call", output_to_operand_aliasing={{1}: (4, {}), {2}: (5, {}), {3}: (6, {}), {4}: (7, {}), {5}... | custom-call | tf_op jit(solution)/shard_map/pallas_call | solution.py:545
  19.9 0.0 collective-permute-done.3.far
  19.9 1.4 %shard_map.47 = (f32[5,8,128]{2,1,0:T(8,128)S(1)}, f32[14,2,160,128]{3,2,1,0:T(8,128)S(1)}, f32[14,2,160,128]{3,2,1,0:T(8,128)S(1)}, f32[14,2,160,128]{3,2,1,0:T...) custom-call(f32[4,128,256]{2,1,0:T(8,128)S(1)} %collective-permute-d, ...), custom_call_target="tpu_custom_call", output_to_operand_aliasing={{1}: (2, {}), {2}: (3, {}), {3}: (4, {}), {4}: (5, {}), {5}... | custom-call | tf_op jit(solution)/shard_map/pallas_call | solution.py:547
  21.3 0.0 collective-permute-done.2.rfc
  21.3 0.7 %shard_map.48 = (f32[1,128]{1,0:T(1,128)S(1)}, f32[14,2,160,128]{3,2,1,0:T(8,128)S(1)}, f32[14,2,160,128]{3,2,1,0:T(8,128)S(1)}, f32[14,2,160,128]{3,2,1,0:T(8,1...) custom-call(f32[4,8,256]{2,1,0:T(8,128)S(1)} %collective-permute-don, ...), custom_call_target="tpu_custom_call", output_to_operand_aliasing={{1}: (2, {}), {2}: (3, {}), {3}: (4, {}), {4}: (5, {}), {5}... | custom-call | tf_op jit(solution)/shard_map/pallas_call | solution.py:549
  22.0 10.7 %all_to_all.5 = f32[32,1,128]{2,1,0:T(1,128)S(1)} all-to-all(f32[32,1,128]{2,1,0:T(1,128)S(1)} %broadcast_in_dim.9), channel_id=1, replica_groups=mesh['gx'=8,'gy'=4] {'gx','gy'}, dimensions={0} | all-to-all | bytes 32768 | tf_op jit(solution)/shard_map/all_to_all | solution.py:555
  32.7 1.8 %last_kernel.1 = (f32[8,128,256]{2,1,0:T(8,128)}, f32[8,128,256]{2,1,0:T(8,128)}) custom-call(f32[32,128]{1,0:T(8,128)S(1)} %bitcast.2, f32[14,2,160,128]{3,2,1,0:T(8,128)S(1)} %get-tuple-element.106.sx, f32[14,2,160,128]{3,2,1,0:T(8,128)S(1)} %get-tuple-element.107.sc, f32[14,2,160,128]{3,2,1,0:T(8,128)S(1)} %get-tuple-element.108.w0, ...), custom_call_target="tpu_custom_call" | custom-call | tf_op jit(solution)/shard_map/last_kernel/pallas_call | solution.py:558
  (1 shorter events, 0.0 us)
Async XLA Ops:
  0.6 1.2 %copy-start = (f32[8,128,256]{2,1,0:T(8,128)S(1)}, f32[8,128,256]{2,1,0:T(8,128)}, u32[]{:S(2)}) copy-start(f32[8,128,256]{2,1,0:T(8,128)} %dens.5) | copy-start | bytes 3145732
  1.9 1.2 %copy-start.2 = (f32[8,128,256]{2,1,0:T(8,128)S(1)}, f32[8,128,256]{2,1,0:T(8,128)}, u32[]{:S(2)}) copy-start(f32[8,128,256]{2,1,0:T(8,128)} %src.5) | copy-start | bytes 3145732
  3.1 8.8 %copy-start.1 = (f32[8,128,256]{2,1,0:T(8,128)S(1)}, f32[8,128,256]{2,1,0:T(8,128)}, u32[]{:S(2)}) copy-start(f32[8,128,256]{2,1,0:T(8,128)} %dens.5) | copy-start | bytes 3145732
  3.1 8.8 %copy-start.3 = (f32[8,128,256]{2,1,0:T(8,128)S(1)}, f32[8,128,256]{2,1,0:T(8,128)}, u32[]{:S(2)}) copy-start(f32[8,128,256]{2,1,0:T(8,128)} %src.5) | copy-start | bytes 3145732
  3.2 14.3 %collective-permute-start.5 = (f32[5,128,256]{2,1,0:T(8,128)S(1)}, f32[5,128,256]{2,1,0:T(8,128)S(1)}, u32[]{:S(2)}, u32[]{:S(2)}) collective-permute-start(f32[5,128,256]{2,1,0:T(8,128)S(1)} %get-tuple-element.60), channel_id=1, source_target_pairs={{0,4},{1,5},{2,6},{3,7},{4,0},{5,1},{6,2},{7,3},{8,12},{9,13},{10,... | collective-permute-start | bytes 1966088 | tf_op jit(solution)/shard_map/ppermute | solution.py:518
  5.2 14.7 %collective-permute-start.3 = (f32[4,128,256]{2,1,0:T(8,128)S(1)}, f32[4,128,256]{2,1,0:T(8,128)S(1)}, u32[]{:S(2)}, u32[]{:S(2)}) collective-permute-start(f32[4,128,256]{2,1,0:T(8,128)S(1)} %load_far_kernel.1), channel_id=1, source_target_pairs={{0,2},{1,3},{2,0},{3,1},{4,8},{5,9},{6,10},{7,11},{8,4},{9,5},{10,... | collective-permute-start | bytes 1572872 | tf_op jit(solution)/shard_map/ppermute | solution.py:518
  7.9 4.0 %collective-permute-start = (f32[5,8,256]{2,1,0:T(8,128)S(1)}, f32[5,8,256]{2,1,0:T(8,128)S(1)}, u32[]{:S(2)}, u32[]{:S(2)}) collective-permute-start(f32[5,8,256]{2,1,0:T(8,128)S(1)} %get-tuple-element.56), channel_id=1, source_target_pairs={{0,1},{1,0},{2,3},{3,2},{4,5},{5,4},{6,7},{7,6},{8,9},{9,8},{10,11... | collective-permute-start | bytes 122888 | tf_op jit(solution)/shard_map/ppermute | solution.py:518
  9.4 2.5 %collective-permute-start.1 = (f32[5,8,256]{2,1,0:T(8,128)S(1)}, f32[5,8,256]{2,1,0:T(8,128)S(1)}, u32[]{:S(2)}, u32[]{:S(2)}) collective-permute-start(f32[5,8,256]{2,1,0:T(8,128)S(1)} %get-tuple-element.57), channel_id=1, source_target_pairs={{0,4},{1,2},{2,1},{3,7},{4,0},{5,6},{6,5},{7,3},{8,12},{9,10},{10,... | collective-permute-start | bytes 122888 | tf_op jit(solution)/shard_map/ppermute | solution.py:518
  12.0 7.2 %collective-permute-start.4 = (f32[4,8,256]{2,1,0:T(8,128)S(1)}, f32[4,8,256]{2,1,0:T(8,128)S(1)}, u32[]{:S(2)}, u32[]{:S(2)}) collective-permute-start(f32[4,8,256]{2,1,0:T(8,128)S(1)} %get-tuple-element.59), channel_id=1, source_target_pairs={{0,4},{1,5},{2,6},{3,7},{4,0},{5,1},{6,2},{7,3},{8,12},{9,13},{10,... | collective-permute-start | bytes 98312 | tf_op jit(solution)/shard_map/ppermute | solution.py:518
  12.0 9.2 %collective-permute-start.2 = (f32[4,8,256]{2,1,0:T(8,128)S(1)}, f32[4,8,256]{2,1,0:T(8,128)S(1)}, u32[]{:S(2)}, u32[]{:S(2)}) collective-permute-start(f32[4,8,256]{2,1,0:T(8,128)S(1)} %get-tuple-element.58), channel_id=1, source_target_pairs={{0,2},{1,3},{2,0},{3,1},{4,8},{5,9},{6,10},{7,11},{8,4},{9,5},{10,... | collective-permute-start | bytes 98312 | tf_op jit(solution)/shard_map/ppermute | solution.py:518
where the time goes:
time: 34.7 us; the launch traced here: 34.5 us
  blocking collectives  10.7 us (31%)
  Pallas kernels  9.76 us (28%)
  starting transfers between devices  8.24 us (24%)
  waiting for transfers between devices  2.52 us (7%)
  local copies, waits for them, and re-layouts  2.46 us (7%)
  between operations  0.74 us (2%)
    all_to_all x1, blocking collectives, shards(): got = lax.all_to_all(sent, both, 0, 0, tiled=True).reshape(n, LANES)  10.7 us
    ppermute x6, starting transfers between devices, send(): return lax.ppermute(value, both, pairs)  8.24 us
    ppermute x6, waiting for transfers between devices, send(): return lax.ppermute(value, both, pairs)  2.52 us
    unnamed x8, local copies, waits for them, and re-layouts  2.45 us
    pallas_call x1, Pallas kernels, shards(): *held, n0, part = call(inner_kernel, 2, (ext,) * 10 + (sums,), 8)(dens, src)  1.97 us
    pallas_call x1, Pallas kernels, shards(): pl.pallas_call(last_kernel, out_shape=(whole, whole), in_specs=[vmem] * 5...  1.76 us
    pallas_call x1, Pallas kernels, shards(): pl.pallas_call(functools.partial(load_far_kernel, sizes), out_shape=few,...  1.43 us
    pallas_call x1, Pallas kernels, shards(): call(far_kernel, 12, (sums,) + (ext,) * 10, 8, input_output_aliases={2 +...  1.41 us
  transfers between devices with their start and end apart: 6, of which 1 were waited for; matrix products, arithmetic and copies ran while one was open for 0% of the time, Pallas kernels for 21%

commit v1 on v0

--- a/solution.py
+++ b/solution.py
@@ -13,7 +13,7 @@
 OFF = 16
 DEEP = 3
 ROWS = 5
-STEP = 2
+STEP = 1
 HALF = TILE // 2
 PART = 16
 SUMS = 5
@@ -315,7 +315,7 @@
     return jnp.where(xodd, 1, 4), jnp.where(xodd, 2, 5), jnp.where(xodd, 3, 6), jnp.where(xodd, par[2], par[3])
 
 
-def inner_kernel(sizes, dens, src, dx, sx, wx, wy, wz, sc, g0, g1, w0, n0, mom):
+def inner_kernel(sizes, dens, src, dx, sx, wx, wy, wz, sc, g0, g1, w0):
     nx, ny, _ = dens.shape
     own = slice(OFF, OFF + ny)
 
@@ -326,10 +326,6 @@
     loop(nx, fill)
     weigh(dx, sx, wx, wy, wz, sc, g0, DEEP + 1, nx - 2, row_tiles(1, ny - 1), unroll=2)
     apply_first(sx, wx, wy, wz, sc, g0, g1, w0, DEEP + 2, nx - 4, row_tiles(2, ny - 2), unroll=4)
-    zero = jnp.zeros((TILE, LANES), jnp.float32)
-    sums = apply_second(sx, wx, wy, wz, sc, g1, w0, n0, DEEP + 3, nx - 6, row_tiles(HALF, ny - HALF), (zero,) * SUMS)
-    for i in range(SUMS):
-        mom[i] = sums[i]
 
 
 def beside_kernel(sizes, near, *refs):
@@ -349,11 +345,12 @@
     clear_plane(g1, jnp.where(xodd, 2, nx + 3), has, row_tiles(2, ny - 2))
 
 
-def inner_second_kernel(sizes, sx, wx, wy, wz, sc, g1, w0, part, n0_in, n0, mom):
+def inner_second_kernel(sizes, sx, wx, wy, wz, sc, g1, w0, n0, mom):
     par = position(sizes)
     nx, ny = sx.shape[0] - 2 * DEEP, sx.shape[2] - 2 * OFF
-    third = jnp.where(par[0] == 1, DEEP, nx)
-    sums = apply_second(sx, wx, wy, wz, sc, g1, w0, n0, third, 3, row_tiles(HALF, ny - HALF), [part[i] for i in range(SUMS)], unroll=3)
+    third = near_side(par)[2]
+    zero = jnp.zeros((TILE, LANES), jnp.float32)
+    sums = apply_second(sx, wx, wy, wz, sc, g1, w0, n0, third, nx - 3, row_tiles(HALF, ny - HALF), (zero,) * SUMS, unroll=5)
     for i in range(SUMS):
         mom[i] = sums[i]
 
@@ -537,10 +534,10 @@
 
     ext = VMEM((nx + 2 * DEEP, nz // LANES, ny + 2 * OFF, LANES), jnp.float32)
     sums = VMEM((SUMS, TILE, LANES), jnp.float32)
-    *held, n0, part = call(inner_kernel, 2, (ext,) * 10 + (sums,), 8)(dens, src)
+    held = call(inner_kernel, 2, (ext,) * 9, 8)(dens, src)
     held = call(beside_kernel, 10, (ext,) * 9, 8, input_output_aliases={1 + k: k for k in range(9)})(near, *held)
     dx, sx, wx, wy, wz, sc, g0, g1, w0 = held
-    n0, part = call(inner_second_kernel, 9, (ext, sums), 8, input_output_aliases={8: 0})(sx, wx, wy, wz, sc, g1, w0, part, n0)
+    n0, part = call(inner_second_kernel, 7, (ext, sums), 8)(sx, wx, wy, wz, sc, g1, w0)
     held = (*held, n0)
     part, *held = call(edge_kernel, 14, (sums,) + (ext,) * 10, 8, input_output_aliases={4 + k: 1 + k for k in range(10)})(
         rxs, rdg, rnc, part, *held)

time: 34.7 us -> 34.6 us (level)
  no operation moved by 1% of the time
where the time goes in v1:
time: 34.6 us; the launch traced here: 34.4 us
  blocking collectives  10.8 us (31%)
  Pallas kernels  9.65 us (28%)
  starting transfers between devices  8.24 us (24%)
  waiting for transfers between devices  2.52 us (7%)
  local copies, waits for them, and re-layouts  2.46 us (7%)
  between operations  0.74 us (2%)
    all_to_all x1, blocking collectives, shards(): got = lax.all_to_all(sent, both, 0, 0, tiled=True).reshape(n, LANES)  10.8 us
    ppermute x6, starting transfers between devices, send(): return lax.ppermute(value, both, pairs)  8.24 us
    ppermute x6, waiting for transfers between devices, send(): return lax.ppermute(value, both, pairs)  2.52 us
    unnamed x8, local copies, waits for them, and re-layouts  2.45 us
    pallas_call x1, Pallas kernels, shards(): pl.pallas_call(last_kernel, out_shape=(whole, whole), in_specs=[vmem] * 5...  1.73 us
    pallas_call x1, Pallas kernels, shards(): held = call(inner_kernel, 2, (ext,) * 9, 8)(dens, src)  1.62 us
    pallas_call x1, Pallas kernels, shards(): pl.pallas_call(functools.partial(load_far_kernel, sizes), out_shape=few,...  1.43 us
    pallas_call x1, Pallas kernels, shards(): call(far_kernel, 12, (sums,) + (ext,) * 10, 8, input_output_aliases={2 +...  1.4 us
  transfers between devices with their start and end apart: 6, of which 1 were waited for; matrix products, arithmetic and copies ran while one was open for 0% of the time, Pallas kernels for 21%

profile of v1, /device:TPU:0, one launch (start us, length us, event | category | flops | bytes accessed | tf_op | source)
XLA Modules:
  0.0 34.4 jit_solution(6663984716006505811)
XLA Ops:
  0.6 0.0 copy-start
  0.6 1.2 %copy-done = f32[8,128,256]{2,1,0:T(8,128)S(1)} copy-done((f32[8,128,256]{2,1,0:T(8,128)S(1)}, f32[8,128,256]{2,1,0:T(8,128)}, u32[]{:S(2)}) %copy-start) | copy-done | bytes 1048600
  1.9 0.0 copy-start.2
  1.9 1.2 %copy-done.2 = f32[8,128,256]{2,1,0:T(8,128)S(1)} copy-done((f32[8,128,256]{2,1,0:T(8,128)S(1)}, f32[8,128,256]{2,1,0:T(8,128)}, u32[]{:S(2)}) %copy-start.2) | copy-done | bytes 1048600
  3.1 0.0 copy-start.1
  3.1 0.0 copy-start.3
  3.1 0.1 shard_map.41
  3.2 0.6 %collective-permute-start.5 = (f32[5,128,256]{2,1,0:T(8,128)S(1)}, f32[5,128,256]{2,1,0:T(8,128)S(1)}, u32[]{:S(2)}, u32[]{:S(2)}) collective-permute-start(f32[5,128,256]{2,1,0:T(8,128)S(1)} %get-tuple-element.58), channel_id=1, source_target_pairs={{0,4},{1,5},{2,6},{3,7},{4,0},{5,1},{6,2},{7,3},{8,12},{9,13},{10,... | collective-permute-start | bytes 1966088 | tf_op jit(solution)/shard_map/ppermute | solution.py:515
  3.7 1.4 %load_far_kernel.1 = f32[4,128,256]{2,1,0:T(8,128)S(1)} custom-call(f32[8,128,256]{2,1,0:T(8,128)} %dens.5, f32[8,128,256]{2,1,0:T(8,128)} %src.5), custom_call_target="tpu_custom_call" | custom-call | tf_op jit(solution)/shard_map/load_far_kernel/pallas_call | solution.py:518
  5.2 2.7 %collective-permute-start.3 = (f32[4,128,256]{2,1,0:T(8,128)S(1)}, f32[4,128,256]{2,1,0:T(8,128)S(1)}, u32[]{:S(2)}, u32[]{:S(2)}) collective-permute-start(f32[4,128,256]{2,1,0:T(8,128)S(1)} %load_far_kernel.1), channel_id=1, source_target_pairs={{0,2},{1,3},{2,0},{3,1},{4,8},{5,9},{6,10},{7,11},{8,4},{9,5},{10,... | collective-permute-start | bytes 1572872 | tf_op jit(solution)/shard_map/ppermute | solution.py:515
  7.9 1.5 %collective-permute-start = (f32[5,8,256]{2,1,0:T(8,128)S(1)}, f32[5,8,256]{2,1,0:T(8,128)S(1)}, u32[]{:S(2)}, u32[]{:S(2)}) collective-permute-start(f32[5,8,256]{2,1,0:T(8,128)S(1)} %get-tuple-element.54), channel_id=1, source_target_pairs={{0,1},{1,0},{2,3},{3,2},{4,5},{5,4},{6,7},{7,6},{8,9},{9,8},{10,11... | collective-permute-start | bytes 122888 | tf_op jit(solution)/shard_map/ppermute | solution.py:515
  9.4 0.0 collective-permute-start.1
  9.4 2.5 %collective-permute-done.rxs = f32[5,8,256]{2,1,0:T(8,128)S(1)} collective-permute-done((f32[5,8,256]{2,1,0:T(8,128)S(1)}, f32[5,8,256]{2,1,0:T(8,128)S(1)}, u32[]{:S(2)}, u32[]{:S(2)}) %collective-permute-start) | collective-permute-done | bytes 40992 | tf_op jit(solution)/shard_map/ppermute | solution.py:515
  11.9 0.0 collective-permute-done.1.rdg
  11.9 0.0 copy-done.1
  11.9 0.0 copy-done.3
  11.9 0.1 shard_map.42
  12.0 0.1 collective-permute-start.4
  12.0 3.4 %collective-permute-start.2 = (f32[4,8,256]{2,1,0:T(8,128)S(1)}, f32[4,8,256]{2,1,0:T(8,128)S(1)}, u32[]{:S(2)}, u32[]{:S(2)}) collective-permute-start(f32[4,8,256]{2,1,0:T(8,128)S(1)} %get-tuple-element.56), channel_id=1, source_target_pairs={{0,2},{1,3},{2,0},{3,1},{4,8},{5,9},{6,10},{7,11},{8,4},{9,5},{10,... | collective-permute-start | bytes 98312 | tf_op jit(solution)/shard_map/ppermute | solution.py:515
  15.4 1.6 %shard_map.43 = (f32[14,2,160,128]{3,2,1,0:T(8,128)S(1)}, f32[14,2,160,128]{3,2,1,0:T(8,128)S(1)}, f32[14,2,160,128]{3,2,1,0:T(8,128)S(1)}, f32[14,2,160,128]{3,...) custom-call(f32[8,128,256]{2,1,0:T(8,128)S(1)} %copy-done.1, ...), custom_call_target="tpu_custom_call" | custom-call | tf_op jit(solution)/shard_map/pallas_call | solution.py:537
  17.1 0.0 collective-permute-done.5.near
  17.1 1.2 %shard_map.44 = (f32[14,2,160,128]{3,2,1,0:T(8,128)S(1)}, f32[14,2,160,128]{3,2,1,0:T(8,128)S(1)}, f32[14,2,160,128]{3,2,1,0:T(8,128)S(1)}, f32[14,2,160,128]{3,...) custom-call(f32[5,128,256]{2,1,0:T(8,128)S(1)} %collective-permute-d, ...), custom_call_target="tpu_custom_call", output_to_operand_aliasing={{0}: (1, {}), {1}: (2, {}), {2}: (3, {}), {3}: (4, {}), {4}... | custom-call | tf_op jit(solution)/shard_map/pallas_call | solution.py:538
  18.3 0.8 %shard_map.45 = (f32[14,2,160,128]{3,2,1,0:T(8,128)S(1)}, f32[5,8,128]{2,1,0:T(8,128)S(1)}) custom-call(f32[14,2,160,128]{3,2,1,0:T(8,128)S(1)} %get-tuple-element.68.sx.refs_1_, f32[14,2,160,128]{3,2,1,0:T(8,128)S(1)} %get-tuple-element.69.wx.refs_2_, f32[14,2,160,128]{3,2,1,0:T(8,128)S(1)} %get-tuple-element.70.wy.refs_3_, ...), custom_call_target="tpu_custom_call" | custom-call | tf_op jit(solution)/shard_map/pallas_call | solution.py:540
  19.1 0.0 collective-permute-done.4.rnc
  19.1 0.7 %shard_map.46 = (f32[5,8,128]{2,1,0:T(8,128)S(1)}, f32[14,2,160,128]{3,2,1,0:T(8,128)S(1)}, f32[14,2,160,128]{3,2,1,0:T(8,128)S(1)}, f32[14,2,160,128]{3,2,1,0:T...) custom-call(f32[5,8,256]{2,1,0:T(8,128)S(1)} %collective-permute-don, ...), custom_call_target="tpu_custom_call", output_to_operand_aliasing={{1}: (4, {}), {2}: (5, {}), {3}: (6, {}), {4}: (7, {}), {5}... | custom-call | tf_op jit(solution)/shard_map/pallas_call | solution.py:542
  19.8 0.0 collective-permute-done.3.far
  19.8 1.4 %shard_map.47 = (f32[5,8,128]{2,1,0:T(8,128)S(1)}, f32[14,2,160,128]{3,2,1,0:T(8,128)S(1)}, f32[14,2,160,128]{3,2,1,0:T(8,128)S(1)}, f32[14,2,160,128]{3,2,1,0:T...) custom-call(f32[4,128,256]{2,1,0:T(8,128)S(1)} %collective-permute-d, ...), custom_call_target="tpu_custom_call", output_to_operand_aliasing={{1}: (2, {}), {2}: (3, {}), {3}: (4, {}), {4}: (5, {}), {5}... | custom-call | tf_op jit(solution)/shard_map/pallas_call | solution.py:544
  21.2 0.0 collective-permute-done.2.rfc
  21.2 0.7 %shard_map.48 = (f32[1,128]{1,0:T(1,128)S(1)}, f32[14,2,160,128]{3,2,1,0:T(8,128)S(1)}, f32[14,2,160,128]{3,2,1,0:T(8,128)S(1)}, f32[14,2,160,128]{3,2,1,0:T(8,1...) custom-call(f32[4,8,256]{2,1,0:T(8,128)S(1)} %collective-permute-don, ...), custom_call_target="tpu_custom_call", output_to_operand_aliasing={{1}: (2, {}), {2}: (3, {}), {3}: (4, {}), {4}: (5, {}), {5}... | custom-call | tf_op jit(solution)/shard_map/pallas_call | solution.py:546
  21.9 10.8 %all_to_all.5 = f32[32,1,128]{2,1,0:T(1,128)S(1)} all-to-all(f32[32,1,128]{2,1,0:T(1,128)S(1)} %broadcast_in_dim.9), channel_id=1, replica_groups=mesh['gx'=8,'gy'=4] {'gx','gy'}, dimensions={0} | all-to-all | bytes 32768 | tf_op jit(solution)/shard_map/all_to_all | solution.py:552
  32.6 1.7 %last_kernel.1 = (f32[8,128,256]{2,1,0:T(8,128)}, f32[8,128,256]{2,1,0:T(8,128)}) custom-call(f32[32,128]{1,0:T(8,128)S(1)} %bitcast.2, f32[14,2,160,128]{3,2,1,0:T(8,128)S(1)} %get-tuple-element.102.sx, f32[14,2,160,128]{3,2,1,0:T(8,128)S(1)} %get-tuple-element.103.sc, f32[14,2,160,128]{3,2,1,0:T(8,128)S(1)} %get-tuple-element.104.w0, ...), custom_call_target="tpu_custom_call" | custom-call | tf_op jit(solution)/shard_map/last_kernel/pallas_call | solution.py:555
  (1 shorter events, 0.0 us)
Async XLA Ops:
  0.6 1.2 %copy-start = (f32[8,128,256]{2,1,0:T(8,128)S(1)}, f32[8,128,256]{2,1,0:T(8,128)}, u32[]{:S(2)}) copy-start(f32[8,128,256]{2,1,0:T(8,128)} %dens.5) | copy-start | bytes 3145732
  1.9 1.2 %copy-start.2 = (f32[8,128,256]{2,1,0:T(8,128)S(1)}, f32[8,128,256]{2,1,0:T(8,128)}, u32[]{:S(2)}) copy-start(f32[8,128,256]{2,1,0:T(8,128)} %src.5) | copy-start | bytes 3145732
  3.1 8.8 %copy-start.1 = (f32[8,128,256]{2,1,0:T(8,128)S(1)}, f32[8,128,256]{2,1,0:T(8,128)}, u32[]{:S(2)}) copy-start(f32[8,128,256]{2,1,0:T(8,128)} %dens.5) | copy-start | bytes 3145732
  3.1 8.8 %copy-start.3 = (f32[8,128,256]{2,1,0:T(8,128)S(1)}, f32[8,128,256]{2,1,0:T(8,128)}, u32[]{:S(2)}) copy-start(f32[8,128,256]{2,1,0:T(8,128)} %src.5) | copy-start | bytes 3145732
  3.2 13.9 %collective-permute-start.5 = (f32[5,128,256]{2,1,0:T(8,128)S(1)}, f32[5,128,256]{2,1,0:T(8,128)S(1)}, u32[]{:S(2)}, u32[]{:S(2)}) collective-permute-start(f32[5,128,256]{2,1,0:T(8,128)S(1)} %get-tuple-element.58), channel_id=1, source_target_pairs={{0,4},{1,5},{2,6},{3,7},{4,0},{5,1},{6,2},{7,3},{8,12},{9,13},{10,... | collective-permute-start | bytes 1966088 | tf_op jit(solution)/shard_map/ppermute | solution.py:515
  5.2 14.6 %collective-permute-start.3 = (f32[4,128,256]{2,1,0:T(8,128)S(1)}, f32[4,128,256]{2,1,0:T(8,128)S(1)}, u32[]{:S(2)}, u32[]{:S(2)}) collective-permute-start(f32[4,128,256]{2,1,0:T(8,128)S(1)} %load_far_kernel.1), channel_id=1, source_target_pairs={{0,2},{1,3},{2,0},{3,1},{4,8},{5,9},{6,10},{7,11},{8,4},{9,5},{10,... | collective-permute-start | bytes 1572872 | tf_op jit(solution)/shard_map/ppermute | solution.py:515
  7.9 4.0 %collective-permute-start = (f32[5,8,256]{2,1,0:T(8,128)S(1)}, f32[5,8,256]{2,1,0:T(8,128)S(1)}, u32[]{:S(2)}, u32[]{:S(2)}) collective-permute-start(f32[5,8,256]{2,1,0:T(8,128)S(1)} %get-tuple-element.54), channel_id=1, source_target_pairs={{0,1},{1,0},{2,3},{3,2},{4,5},{5,4},{6,7},{7,6},{8,9},{9,8},{10,11... | collective-permute-start | bytes 122888 | tf_op jit(solution)/shard_map/ppermute | solution.py:515
  9.4 2.5 %collective-permute-start.1 = (f32[5,8,256]{2,1,0:T(8,128)S(1)}, f32[5,8,256]{2,1,0:T(8,128)S(1)}, u32[]{:S(2)}, u32[]{:S(2)}) collective-permute-start(f32[5,8,256]{2,1,0:T(8,128)S(1)} %get-tuple-element.55), channel_id=1, source_target_pairs={{0,4},{1,2},{2,1},{3,7},{4,0},{5,6},{6,5},{7,3},{8,12},{9,10},{10,... | collective-permute-start | bytes 122888 | tf_op jit(solution)/shard_map/ppermute | solution.py:515
  12.0 7.1 %collective-permute-start.4 = (f32[4,8,256]{2,1,0:T(8,128)S(1)}, f32[4,8,256]{2,1,0:T(8,128)S(1)}, u32[]{:S(2)}, u32[]{:S(2)}) collective-permute-start(f32[4,8,256]{2,1,0:T(8,128)S(1)} %get-tuple-element.57), channel_id=1, source_target_pairs={{0,4},{1,5},{2,6},{3,7},{4,0},{5,1},{6,2},{7,3},{8,12},{9,13},{10,... | collective-permute-start | bytes 98312 | tf_op jit(solution)/shard_map/ppermute | solution.py:515
  12.0 9.2 %collective-permute-start.2 = (f32[4,8,256]{2,1,0:T(8,128)S(1)}, f32[4,8,256]{2,1,0:T(8,128)S(1)}, u32[]{:S(2)}, u32[]{:S(2)}) collective-permute-start(f32[4,8,256]{2,1,0:T(8,128)S(1)} %get-tuple-element.56), channel_id=1, source_target_pairs={{0,2},{1,3},{2,0},{3,1},{4,8},{5,9},{6,10},{7,11},{8,4},{9,5},{10,... | collective-permute-start | bytes 98312 | tf_op jit(solution)/shard_map/ppermute | solution.py:515
